TPU v7x, 32 devices: a whole 2x2x4 slice. The times are simulated.
32 devices in a mesh: groups: 2 (over x), seq: 16 (over z, y, core).
Axes of the slice: x: 2, y: 2, z: 4, core: 2. Of those that a mesh axis runs over, the one named last changes fastest.
Arguments:
- query_in: bfloat16 [4096, 4096], P(('groups', 'seq')), parts along dimension 0, may hold values from -6 to 6
- key_in: bfloat16 [4096, 4096], P(('groups', 'seq')), parts along dimension 0, may hold values from -6 to 6
- value_in: bfloat16 [4096, 4096], P(('groups', 'seq')), parts along dimension 0, may hold values from -6 to 6
- long_filter: bfloat16 [2048, 4096], P('seq'), may hold values from -0.4 to 0.4
- short_weight: float32 [3, 3, 4096], replicated, may hold values from -3 to 3
- skip_gain: float32 [4096], replicated, may hold values from 0.5 to 1.5
Outputs:
- gated_out: bfloat16 [4096, 4096], P(('groups', 'seq')), parts along dimension 0
There are 2 independent parts, one for each index of `groups`. A program takes and returns all parts, laid end to end along the dimension named above; an argument that names none is the same for every part. Nothing has to cross between parts.
All inputs are finite; a program needn't handle non-finite values.
Results may differ from a plain program's by a relative error of at most 0.0052.
Values may be sent and summed in bfloat16 or wider, within the bound.
No kernel may reach another device: no remote copies, remote signals or barrier semaphores. Data moves between devices by JAX's collectives and lax.ppermute only.
A program may use at most 128 MiB of HBM per device.

v0:
```python
import math
import jax
import jax.numpy as jnp
from jax import lax
from jax.sharding import PartitionSpec as P

PRECISE = lax.Precision.HIGHEST


def from_behind(value, axis, steps):
    count = lax.axis_size(axis)
    initial, last = (max(0, -steps), min(count, count - steps))
    return lax.ppermute(value, axis, [(source, source + steps) for source in range(initial, last)])


def featurize(own_rows, earlier, taps_weight):
    rim_rows = earlier.shape[0]
    row_count = own_rows.shape[0]
    extended = jnp.concatenate([earlier, own_rows], axis=0).astype(jnp.float32)
    result = jnp.zeros(own_rows.shape, jnp.float32)
    for offset in range(rim_rows + 1):
        result = (
            result
            + taps_weight[offset] * extended[rim_rows - offset : rim_rows - offset + row_count]
        )
    return result


def phase_pair(left_index, right_index, modulus):
    product_index = left_index[:, None] * right_index[None, :] % modulus
    angle = product_index.astype(jnp.float32) * (2.0 * math.pi / modulus)
    return (jnp.cos(angle), jnp.sin(angle))


def block_forward(real_blocks):
    blocks = real_blocks.shape[0]
    flat_values = real_blocks.reshape(blocks, -1)
    cosine_table, sine_table = phase_pair(
        jnp.arange(2 * blocks, dtype=jnp.int32), jnp.arange(blocks, dtype=jnp.int32), 2 * blocks
    )
    joint_table = jnp.concatenate([cosine_table, -sine_table], axis=0)
    stacked = jnp.dot(joint_table, flat_values, precision=PRECISE)
    return stacked.reshape((2, 2 * blocks) + real_blocks.shape[1:])


def apply_twiddle(stacked, freq_index, row_index, modulus, direction):
    cosine_table, sine_table = phase_pair(freq_index, row_index, modulus)
    cosine_table = cosine_table[:, :, None]
    sine_table = direction * sine_table[:, :, None]
    out_real = stacked[0] * cosine_table + stacked[1] * sine_table
    out_imaginary = stacked[1] * cosine_table - stacked[0] * sine_table
    return jnp.stack([out_real, out_imaginary])


def row_transform(stacked, direction):
    length = stacked.shape[2]
    row_index = jnp.arange(length, dtype=jnp.int32)
    cosine_table, sine_table = phase_pair(row_index, row_index, length)
    sine_table = direction * sine_table
    upper_table = jnp.stack([cosine_table, sine_table], axis=1)
    lower_table = jnp.stack([-sine_table, cosine_table], axis=1)
    full_table = jnp.stack([upper_table, lower_table])
    return jnp.einsum("ymxn,xknc->ykmc", full_table, stacked, precision=PRECISE)


def block_inverse(stacked, factor):
    double_count = stacked.shape[1]
    blocks = double_count // 2
    cosine_table, sine_table = phase_pair(
        jnp.arange(blocks, dtype=jnp.int32), jnp.arange(double_count, dtype=jnp.int32), double_count
    )
    joint_table = jnp.concatenate([cosine_table, -sine_table], axis=1)
    flat_values = stacked.reshape(2 * double_count, -1)
    result = jnp.dot(joint_table, flat_values, precision=PRECISE) * factor
    return result.reshape((blocks,) + stacked.shape[2:])


def spectral_product(stacked, width):
    spectra = row_transform(stacked, 1.0)
    data_real = spectra[0, ..., :width]
    kernel_real = spectra[0, ..., width:]
    data_imaginary = spectra[1, ..., :width]
    kernel_imaginary = spectra[1, ..., width:]
    joint = jnp.stack(
        [
            data_real * kernel_real - data_imaginary * kernel_imaginary,
            data_real * kernel_imaginary + data_imaginary * kernel_real,
        ]
    )
    return row_transform(joint, -1.0)


def along_rows(product, long_filter):
    blocks = lax.axis_size("seq")
    device_index = lax.axis_index("seq")
    row_count, channels = product.shape
    row_share = row_count // blocks
    full_length = 2 * blocks * row_count
    data_parts, kernel_parts = (
        lax.all_to_all(
            product.reshape(1, row_count, channels), "seq", split_axis=1, concat_axis=0, tiled=True
        ),
        lax.all_to_all(
            long_filter.reshape(1, row_count, channels),
            "seq",
            split_axis=1,
            concat_axis=0,
            tiled=True,
        ),
    )
    joined = jnp.concatenate([data_parts, kernel_parts], axis=2).astype(jnp.float32)
    freq_all = jnp.arange(2 * blocks, dtype=jnp.int32)
    local_rows = device_index * row_share + jnp.arange(row_share, dtype=jnp.int32)
    spectra = apply_twiddle(block_forward(joined), freq_all, local_rows, full_length, 1.0)
    spectra = lax.all_to_all(spectra, "seq", split_axis=1, concat_axis=2, tiled=True)
    joint = spectral_product(spectra, channels)
    own_freq = device_index * 2 + jnp.arange(2, dtype=jnp.int32)
    whole_rows = jnp.arange(row_count, dtype=jnp.int32)
    joint = apply_twiddle(joint, own_freq, whole_rows, full_length, -1.0)
    joint = lax.all_to_all(
        joint.astype(jnp.bfloat16), "seq", split_axis=2, concat_axis=1, tiled=True
    ).astype(joint.dtype)
    convolved = block_inverse(joint, 1.0 / full_length).astype(jnp.bfloat16)
    convolved = lax.all_to_all(convolved, "seq", split_axis=0, concat_axis=1, tiled=True)
    return convolved.reshape(row_count, channels)


def on_device(query_in, key_in, value_in, long_filter, short_weight, skip_gain):
    rim_rows = short_weight.shape[1] - 1
    last_rows = jnp.stack([query_in[-rim_rows:], key_in[-rim_rows:], value_in[-rim_rows:]])
    earlier = from_behind(last_rows, "seq", 1)
    q_short = featurize(query_in, earlier[0], short_weight[0])
    k_short = featurize(key_in, earlier[1], short_weight[1])
    v_short = featurize(value_in, earlier[2], short_weight[2])
    product = (k_short * v_short).astype(jnp.bfloat16)
    product_wide = lax.optimization_barrier(product).astype(jnp.float32)
    convolved = along_rows(product, long_filter)
    gated_out = q_short * (convolved.astype(jnp.float32) + skip_gain * product_wide)
    return gated_out.astype(jnp.bfloat16)


def solution(mesh):
    placed = (
        P(("groups", "seq"), None),
        P(("groups", "seq"), None),
        P(("groups", "seq"), None),
        P("seq", None),
        P(),
        P(),
    )
    return jax.shard_map(
        on_device, mesh=mesh, in_specs=placed, out_specs=P(("groups", "seq"), None), check_vma=False
    )
```

profile of v0, /device:TPU:9, one launch (start us, length us, event | category | flops | bytes accessed | tf_op | source)
XLA Modules:
  0.0 698.6 jit_solution(10720077850557271215)
XLA Ops:
  0.0 0.9 slice_bitcast_fusion.5
  0.9 0.9 slice_bitcast_fusion.3
  1.8 0.1 pad_maximum_fusion.7
  1.9 3.7 collective-permute-start
  5.6 3.6 copy.66
  9.2 0.0 copy-start.2
  9.2 0.5 broadcast.416
  9.7 7.0 %reduce = bf16[128,4096]{1,0:T(8,128)(2,1)S(1)} reduce(bf16[128,1,4096]{2,1,0:T(2,128)(2,1)S(1)} %bitcast.152, bf16[]{:T(256)} %broadcast.416), dimensions={1}, to_apply=%bitcast.138.reduce_sub_computation | reduce | bytes 2097154
  16.7 0.0 copy-start
  16.8 0.0 copy-start.1
  16.8 1.9 reshape.316
  18.7 5.7 all-to-all-start.1
  24.4 0.0 copy-done.2
  24.4 0.1 fusion.82
  24.5 0.0 collective-permute-done
  24.6 0.0 copy-done
  24.6 0.3 maximum_convert_fusion.1
  24.9 0.3 maximum_convert_fusion.2
  25.2 1.3 fusion.18
  26.5 2.4 copy.67
  28.9 8.0 %reduce.1 = bf16[128,4096]{1,0:T(8,128)(2,1)} reduce(bf16[128,1,4096]{2,1,0:T(2,128)(2,1)S(1)} %bitcast.154, bf16[]{:T(256)} %broadcast.416), dimensions={1}, to_apply=%bitcast.139.reduce_sub_computation | reduce | bytes 2097154
  36.9 2.9 reshape.318
  39.8 9.3 %all-to-all-done.1 = bf16[16,2,16384]{2,1,0:T(2,128)(2,1)} async-done(((bf16[16,2,16384]{2,1,0:T(2,128)(2,1)}), bf16[16,2,16384]{2,1,0:T(2,128)(2,1)}, u32[]{:S(2)}, u32[]{:S(2)}) %all-to-all-start.1) | async-done | bytes 1048608 | tf_op jit(solution)/shard_map/all_to_all | solution.py:103
  49.2 5.3 all-to-all-start
  54.5 0.1 sine_negate_fusion
  54.5 0.1 fusion.64
  54.6 4.3 reshape.317
  59.0 2.1 copy.64
  61.1 18.2 %all-to-all-done = bf16[16,2,16384]{2,1,0:T(2,128)(2,1)} async-done(((bf16[16,2,16384]{2,1,0:T(2,128)(2,1)}), bf16[16,2,16384]{2,1,0:T(2,128)(2,1)}, u32[]{:S(2)}, u32[]{:S(2)}) %all-to-all-start) | async-done | bytes 1048608 | tf_op jit(solution)/shard_map/all_to_all | solution.py:100
  79.3 4.3 reshape.319
  83.6 1.1 copy.65
  84.7 1.4 pad_maximum_fusion.2
  86.1 1.2 copy.46
  87.3 6.8 fusion.59
  94.1 6.5 fusion.81
  100.6 8.2 %copy.48 = f32[4,8,8,8192]{3,2,1,0:T(8,128)S(1)} copy(f32[4,8,8,8192]{3,1,2,0:T(8,128)} %bitcast.145) | data formatting | bytes 16777216
  108.8 8.2 %copy.47 = f32[4,8,8,8192]{3,2,1,0:T(8,128)S(1)} copy(f32[4,8,8,8192]{3,1,2,0:T(8,128)} %bitcast.144) | data formatting | bytes 16777216
  117.1 6.9 fusion.8
  124.0 11.5 %pad_maximum_fusion = f32[2,32,8,8192]{3,2,0,1:T(8,128)} fusion(f32[1,32,8,8192]{3,2,0,1:T(8,128)} %get-tuple-element.6, f32[1,32,8,8192]{3,2,0,1:T(8,128)} %get-tuple-element.5), kind=kLoop, calls=%fused_computation.2 | loop fusion | flops 4194304 | bytes 33554432 | tf_op jit(solution)/shard_map/stack | solution.py:52
  135.5 5.5 all-to-all-start.2
  141.0 0.3 fusion.43
  141.3 0.3 broadcast_multiply_fusion
  141.5 0.3 fusion.41
  141.9 0.1 fusion.76
  142.0 358.8 %all-to-all-done.2 = f32[2,32,8,8192]{3,2,0,1:T(8,128)} async-done(((f32[2,32,8,8192]{3,2,0,1:T(8,128)}), f32[2,32,8,8192]{3,2,0,1:T(8,128)}, u32[]{:S(2)}, u32[]{:S(2)}) %all-to-all-start.2) | async-done | bytes 16777248 | tf_op jit(solution)/shard_map/all_to_all | solution.py:115
  500.8 30.7 %fusion.3 = f32[2,2,128,8192]{2,3,0,1:T(8,128)S(1)} fusion(f32[1,128,2,128]{3,1,2,0:T(8,128)S(1)} %get-tuple-element.24, f32[1,128,2,128]{3,1,2,0:T(8,128)S(1)} %get-tuple-element.25, f32[2,2,16,8,8192]{4,3,0,1,2:T(8,128)} %bitcast.23), kind=kOutput, calls=%fused_computation.6 | convolution fusion | flops 12884967424 | bytes 33816576 | tf_op jit(solution)/shard_map/ymxn,xknc->ykmc/dot_general | solution.py:63
  531.5 1.1 multiply_subtract_fusion
  532.6 6.7 fusion.15
  539.3 1.1 add_convert_fusion
  540.4 2.4 pad_maximum_fusion.1
  542.8 11.2 %copy.34 = bf16[2,2,128,4096]{3,0,1,2:T(2,128)(2,1)} copy(bf16[2,2,128,4096]{2,3,0,1:T(8,128)(2,1)} %pad_maximum_fusion.1) | data formatting | bytes 8388608 | tf_op jit(solution)/shard_map/stack | solution.py:52
  554.0 7.4 %all-to-all-start.3 = ((bf16[2,2,128,4096]{3,0,1,2:T(2,128)(2,1)}), bf16[2,2,128,4096]{3,0,1,2:T(2,128)(2,1)}, u32[]{:S(2)}, u32[]{:S(2)}) async-start(bf16[2,2,128,4096]{3,0,1,2:T(2,128)(2,1)} %copy.34), calls=%async_computation.3 | async-start | bytes 8388608 | tf_op jit(solution)/shard_map/all_to_all | solution.py:120
  561.5 0.1 sine_negate_fusion.1
  561.5 90.1 %all-to-all-done.3 = bf16[2,2,128,4096]{3,0,1,2:T(2,128)(2,1)} async-done(((bf16[2,2,128,4096]{3,0,1,2:T(2,128)(2,1)}), bf16[2,2,128,4096]{3,0,1,2:T(2,128)(2,1)}, u32[]{:S(2)}, u32[]{:S(2)}) %all-to-all-start.3) | async-done | bytes 4194336 | tf_op jit(solution)/shard_map/all_to_all | solution.py:120
  651.6 5.1 copy.63
  656.7 0.5 copy.36
  657.2 2.6 copy.49
  659.8 1.8 fusion
  661.6 0.0 copy-start.3
  661.6 1.5 copy.50
  663.2 7.1 %all-to-all-start.4 = ((bf16[16,8,4096]{2,1,0:T(8,128)(2,1)}), bf16[16,8,4096]{2,1,0:T(8,128)(2,1)}, u32[]{:S(2)}, u32[]{:S(2)}) async-start(bf16[16,8,4096]{2,1,0:T(8,128)(2,1)} %bitcast.63), calls=%async_computation.4 | async-start | bytes 2097152 | tf_op jit(solution)/shard_map/all_to_all | solution.py:124
  670.3 1.5 maximum_convert_fusion
  671.8 23.4 %all-to-all-done.4 = bf16[16,8,4096]{2,1,0:T(8,128)(2,1)} async-done(((bf16[16,8,4096]{2,1,0:T(8,128)(2,1)}), bf16[16,8,4096]{2,1,0:T(8,128)(2,1)}, u32[]{:S(2)}, u32[]{:S(2)}) %all-to-all-start.4) | async-done | bytes 1048608 | tf_op jit(solution)/shard_map/all_to_all | solution.py:124
  695.2 3.2 fusion.24
  (6 shorter events, 0.1 us)
Async XLA Ops:
  1.9 22.6 %collective-permute-start = (bf16[3,2,4096]{2,1,0:T(2,128)(2,1)S(1)}, bf16[3,2,4096]{2,1,0:T(2,128)(2,1)S(1)}, u32[]{:S(2)}, u32[]{:S(2)}) collective-permute-start(bf16[3,2,4096]{2,1,0:T(2,128)(2,1)S(1)} %pad_maximum_fusion.7), channel_id=1, source_target_pairs={{0,1},{1,2},{2,3},{3,4},{4,5},{5,6},{6,7},{7,8},{8,9},{9,10},{10,1... | collective-permute-start | bytes 147464 | tf_op jit(solution)/shard_map/ppermute | solution.py:13
  9.2 15.2 %copy-start.2 = (f32[3,3,4096]{2,1,0:T(4,128)S(1)}, f32[3,3,4096]{2,1,0:T(4,128)}, u32[]{:S(2)}) copy-start(f32[3,3,4096]{2,1,0:T(4,128)} %param.10) | copy-start | bytes 442372
  16.7 7.8 %copy-start = (bf16[128,4096]{1,0:T(8,128)(2,1)S(1)}, bf16[128,4096]{1,0:T(8,128)(2,1)}, u32[]{:S(2)}) copy-start(bf16[128,4096]{1,0:T(8,128)(2,1)} %param.7) | copy-start | bytes 3145732
  16.8 8.1 %copy-start.1 = (bf16[128,4096]{1,0:T(8,128)(2,1)S(1)}, bf16[128,4096]{1,0:T(8,128)(2,1)}, u32[]{:S(2)}) copy-start(bf16[128,4096]{1,0:T(8,128)(2,1)} %param.8) | copy-start | bytes 3145732
  18.7 30.5 %all-to-all-start.1 = ((bf16[16,2,16384]{2,1,0:T(2,128)(2,1)}), bf16[16,2,16384]{2,1,0:T(2,128)(2,1)}, u32[]{:S(2)}, u32[]{:S(2)}) async-start(bf16[16,2,16384]{2,1,0:T(2,128)(2,1)} %reshape.316), calls=%async_computation.1 | async-start | bytes 2097152 | tf_op jit(solution)/shard_map/all_to_all | solution.py:103
  49.2 30.1 %all-to-all-start = ((bf16[16,2,16384]{2,1,0:T(2,128)(2,1)}), bf16[16,2,16384]{2,1,0:T(2,128)(2,1)}, u32[]{:S(2)}, u32[]{:S(2)}) async-start(bf16[16,2,16384]{2,1,0:T(2,128)(2,1)} %reshape.318), calls=%async_computation | async-start | bytes 2097152 | tf_op jit(solution)/shard_map/all_to_all | solution.py:100
  135.5 365.3 %all-to-all-start.2 = ((f32[2,32,8,8192]{3,2,0,1:T(8,128)}), f32[2,32,8,8192]{3,2,0,1:T(8,128)}, u32[]{:S(2)}, u32[]{:S(2)}) async-start(f32[2,32,8,8192]{3,2,0,1:T(8,128)} %pad_maximum_fusion), calls=%async_computation.2 | async-start | bytes 33554432 | tf_op jit(solution)/shard_map/all_to_all | solution.py:115
  554.0 97.6 %all-to-all-start.3 = ((bf16[2,2,128,4096]{3,0,1,2:T(2,128)(2,1)}), bf16[2,2,128,4096]{3,0,1,2:T(2,128)(2,1)}, u32[]{:S(2)}, u32[]{:S(2)}) async-start(bf16[2,2,128,4096]{3,0,1,2:T(2,128)(2,1)} %copy.34), calls=%async_computation.3 | async-start | bytes 8388608 | tf_op jit(solution)/shard_map/all_to_all | solution.py:120
  661.6 33.6 %copy-start.3 = (f32[4096]{0:T(1024)S(1)}, f32[4096]{0:T(1024)}, u32[]{:S(2)}) copy-start(f32[4096]{0:T(1024)} %param.11) | copy-start | bytes 49156
  663.2 32.0 %all-to-all-start.4 = ((bf16[16,8,4096]{2,1,0:T(8,128)(2,1)}), bf16[16,8,4096]{2,1,0:T(8,128)(2,1)}, u32[]{:S(2)}, u32[]{:S(2)}) async-start(bf16[16,8,4096]{2,1,0:T(8,128)(2,1)} %bitcast.63), calls=%async_computation.4 | async-start | bytes 2097152 | tf_op jit(solution)/shard_map/all_to_all | solution.py:124
where the time goes:
time: 707 us; the launch traced here: 699 us
  waiting for transfers between devices  500 us (71%)
  local copies, waits for them, and re-layouts  70.2 us (10%)
  other arithmetic  47.2 us (7%)
  matrix products  46.1 us (7%)
  starting transfers between devices  34.7 us (5%)
    all_to_all x1, waiting for transfers between devices, along_rows(): lax.all_to_all(spectra, 'seq', split_axis=1, concat_axis=2, tiled=True)  359 us
    all_to_all x1, waiting for transfers between devices, along_rows(): lax.all_to_all(joint.astype(jnp.bfloat16), 'seq', split_axis=2, concat_ax...  90.1 us
    unnamed x20, local copies, waits for them, and re-layouts  39.1 us
    dot_general x2, matrix products, row_transform(): return jnp.einsum('ymxn,xknc->ykmc', full_table, stacked, precision=PRECISE)  37.4 us
    all_to_all x1, waiting for transfers between devices, along_rows(): lax.all_to_all(convolved, 'seq', split_axis=0, concat_axis=1, tiled=True)  23.4 us
    all_to_all x1, waiting for transfers between devices, along_rows(): lax.all_to_all(product.reshape(1, row_count, channels), 'seq', split_axis...  18.2 us
    unnamed x2, other arithmetic  15 us
  transfers between devices with their start and end apart: 6, of which 5 were waited for; matrix products, arithmetic and copies ran while one was open for 5% of the time, Pallas kernels for 0%

commit v1 on v0

--- a/solution.py
+++ b/solution.py
@@ -112,7 +112,19 @@
     freq_all = jnp.arange(2 * blocks, dtype=jnp.int32)
     local_rows = device_index * row_share + jnp.arange(row_share, dtype=jnp.int32)
     spectra = apply_twiddle(block_forward(joined), freq_all, local_rows, full_length, 1.0)
-    spectra = lax.all_to_all(spectra, "seq", split_axis=1, concat_axis=2, tiled=True)
+    ways, here = (lax.axis_size("seq"), lax.axis_index("seq"))
+    width_2 = spectra.shape[1] // ways
+    shape = list(spectra.shape)
+    shape[1] = width_2
+    height = shape[2]
+    shape[2] = height * ways
+    full = jnp.zeros(shape, spectra.dtype)
+    for mask in range(ways):
+        part = lax.dynamic_slice_in_dim(spectra, (here ^ mask) * width_2, width_2, axis=1)
+        if mask:
+            part = lax.ppermute(part, "seq", [(d, d ^ mask) for d in range(ways)])
+        full = lax.dynamic_update_slice_in_dim(full, part, (here ^ mask) * height, axis=2)
+    spectra = full
     joint = spectral_product(spectra, channels)
     own_freq = device_index * 2 + jnp.arange(2, dtype=jnp.int32)
     whole_rows = jnp.arange(row_count, dtype=jnp.int32)

time: 707 us -> 2250 us (3.18); the launches traced: 699 us -> 2210 us
  local copies, waits for them, and re-layouts: 70.2 us -> 1690 us
  waiting for transfers between devices: 500 us -> 389 us
    dynamic_update_slice x0 -> x16, local copies, waits for them, and re-layouts: none -> 1460 us  [along_rows(): lax.dynamic_update_slice_in_dim(full, part, (here ^ mask) * height, axis=2)]
    all_to_all x1 -> x0, waiting for transfers between devices: 359 us -> none  [along_rows(): lax.all_to_all(spectra, 'seq', split_axis=1, concat_axis=2, tiled=True)]
    ppermute x0 -> x15, waiting for transfers between devices: none -> 246 us  [along_rows(): part = lax.ppermute(part, 'seq', [(d, d ^ mask) for d in range(ways)])]
    ppermute x0 -> x15, local copies, waits for them, and re-layouts: none -> 138 us  [along_rows(): part = lax.ppermute(part, 'seq', [(d, d ^ mask) for d in range(ways)])]
  transfers between devices with their start and end apart: 6 -> 20, of which waited for: 5 -> 10; matrix products, arithmetic and copies ran while one was open for 5% -> 71% of each run, Pallas kernels for 0% -> 0%
where the time goes in v1:
time: 2250 us; the launch traced here: 2210 us
  local copies, waits for them, and re-layouts  1690 us (75%)
  waiting for transfers between devices  389 us (17%)
  starting transfers between devices  50 us (2%)
  other arithmetic  45.7 us (2%)
  matrix products  32.5 us (1%)
    dynamic_update_slice x16, local copies, waits for them, and re-layouts, along_rows(): lax.dynamic_update_slice_in_dim(full, part, (here ^ mask) * height, axis=2)  1460 us
    ppermute x15, waiting for transfers between devices, along_rows(): part = lax.ppermute(part, 'seq', [(d, d ^ mask) for d in range(ways)])  246 us
    ppermute x15, local copies, waits for them, and re-layouts, along_rows(): part = lax.ppermute(part, 'seq', [(d, d ^ mask) for d in range(ways)])  138 us
    all_to_all x1, waiting for transfers between devices, along_rows(): lax.all_to_all(joint.astype(jnp.bfloat16), 'seq', split_axis=2, concat_ax...  90.1 us
  transfers between devices with their start and end apart: 20, of which 10 were waited for; matrix products, arithmetic and copies ran while one was open for 71% of the time, Pallas kernels for 0%

profile of v1, /device:TPU:9, one launch (start us, length us, event | category | flops | bytes accessed | tf_op | source)
XLA Modules:
  0.0 2209.3 jit_solution(1518289455778628274)
XLA Ops:
  1.9 3.7 collective-permute-start
  5.6 3.6 copy.76
  9.8 7.1 reduce
  18.8 5.4 all-to-all-start.1
  30.8 8.0 reduce.1
  38.8 2.9 reshape.318
  41.8 7.1 all-to-all-done.1
  48.9 5.3 all-to-all-start
  56.7 22.3 %all-to-all-done = bf16[16,2,16384]{2,1,0:T(2,128)(2,1)} async-done(((bf16[16,2,16384]{2,1,0:T(2,128)(2,1)}), bf16[16,2,16384]{2,1,0:T(2,128)(2,1)}, u32[]{:S(2)}, u32[]{:S(2)}) %all-to-all-start) | async-done | bytes 1048608 | tf_op jit(solution)/shard_map/all_to_all | solution.py:100
  79.0 4.3 reshape.319
  85.8 6.8 fusion.71
  92.6 6.7 fusion.93
  99.4 11.7 copy.65
  111.1 8.2 copy.64
  119.2 7.2 fusion.7
  136.6 4.1 fusion.36
  143.2 10.2 collective-permute-done.2
  155.4 21.4 collective-permute-done.3
  181.4 62.7 %collective-permute-done.6 = f32[2,2,8,8192]{3,2,1,0:T(8,128)} collective-permute-done((f32[2,2,8,8192]{3,2,1,0:T(8,128)S(1)}, f32[2,2,8,8192]{3,2,1,0:T(8,128)}, u32[]{:S(2)}, u32[]{:S(2)}) %collective-permute-start.6) | collective-permute-done | bytes 1048608 | tf_op jit(solution)/shard_map/ppermute | solution.py:125
  244.1 4.3 collective-permute-start.11
  248.5 18.1 collective-permute-done.7
  271.4 131.6 %collective-permute-done.10 = f32[2,2,8,8192]{3,2,1,0:T(8,128)} collective-permute-done((f32[2,2,8,8192]{3,2,1,0:T(8,128)S(1)}, f32[2,2,8,8192]{3,2,1,0:T(8,128)}, u32[]{:S(2)}, u32[]{:S(2)}) %collective-permute-start.10) | collective-permute-done | bytes 1048608 | tf_op jit(solution)/shard_map/ppermute | solution.py:125
  406.6 8.6 copy.38
  415.2 6.9 broadcast_in_dim.2
  422.0 92.3 %dynamic_update_slice.48 = f32[2,2,128,8192]{2,3,0,1:T(8,128)} dynamic-update-slice(f32[2,2,128,8192]{2,3,0,1:T(8,128)} %broadcast_in_dim.2, f32[2,2,8,8192]{2,3,0,1:T(8,128)} %copy.38, s32[]{:T(128)} %constant.44.clone.1, s32[]{:T(128)} %constant.44.clone.1, s32[]{:T(128)S(6)} %select_n.188, s32[]{:T(128)} %constant.44.clone.1) | dynamic-update-slice | bytes 2097156 | tf_op jit(solution)/shard_map/dynamic_update_slice | solution.py:126
  514.3 9.3 copy.39
  523.6 92.3 %dynamic_update_slice.49 = f32[2,2,128,8192]{2,3,0,1:T(8,128)} dynamic-update-slice(f32[2,2,128,8192]{2,3,0,1:T(8,128)} %dynamic_update_slice.48, f32[2,2,8,8192]{2,3,0,1:T(8,128)} %copy.39, s32[]{:T(128)} %constant.44.clone.1, s32[]{:T(128)} %constant.44.clone.1, s32[]{:T(128)S(6)} %select_n.190, s32[]{:T(128)} %constant.44.clone.1) | dynamic-update-slice | bytes 2097156 | tf_op jit(solution)/shard_map/dynamic_update_slice | solution.py:126
  615.8 9.3 copy.40
  625.1 92.3 %dynamic_update_slice.50 = f32[2,2,128,8192]{2,3,0,1:T(8,128)} dynamic-update-slice(f32[2,2,128,8192]{2,3,0,1:T(8,128)} %dynamic_update_slice.49, f32[2,2,8,8192]{2,3,0,1:T(8,128)} %copy.40, s32[]{:T(128)} %constant.44.clone.1, s32[]{:T(128)} %constant.44.clone.1, s32[]{:T(128)S(6)} %select_n.192, s32[]{:T(128)} %constant.44.clone.1) | dynamic-update-slice | bytes 2097156 | tf_op jit(solution)/shard_map/dynamic_update_slice | solution.py:126
  717.4 8.6 copy.41
  725.9 92.3 %dynamic_update_slice.51 = f32[2,2,128,8192]{2,3,0,1:T(8,128)} dynamic-update-slice(f32[2,2,128,8192]{2,3,0,1:T(8,128)} %dynamic_update_slice.50, f32[2,2,8,8192]{2,3,0,1:T(8,128)} %copy.41, s32[]{:T(128)} %constant.44.clone.1, s32[]{:T(128)} %constant.44.clone.1, s32[]{:T(128)S(6)} %select_n.194, s32[]{:T(128)} %constant.44.clone.1) | dynamic-update-slice | bytes 2097156 | tf_op jit(solution)/shard_map/dynamic_update_slice | solution.py:126
  818.2 8.6 copy.42
  826.8 92.3 %dynamic_update_slice.52 = f32[2,2,128,8192]{2,3,0,1:T(8,128)} dynamic-update-slice(f32[2,2,128,8192]{2,3,0,1:T(8,128)} %dynamic_update_slice.51, f32[2,2,8,8192]{2,3,0,1:T(8,128)} %copy.42, s32[]{:T(128)} %constant.44.clone.1, s32[]{:T(128)} %constant.44.clone.1, s32[]{:T(128)S(6)} %select_n.196, s32[]{:T(128)} %constant.44.clone.1) | dynamic-update-slice | bytes 2097156 | tf_op jit(solution)/shard_map/dynamic_update_slice | solution.py:126
  919.0 9.3 copy.43
  928.3 79.2 %dynamic_update_slice.53 = f32[2,2,128,8192]{2,3,0,1:T(8,128)} dynamic-update-slice(f32[2,2,128,8192]{2,3,0,1:T(8,128)} %dynamic_update_slice.52, f32[2,2,8,8192]{2,3,0,1:T(8,128)} %copy.43, s32[]{:T(128)} %constant.44.clone.1, s32[]{:T(128)} %constant.44.clone.1, s32[]{:T(128)S(6)} %select_n.198, s32[]{:T(128)} %constant.44.clone.1) | dynamic-update-slice | bytes 2097156 | tf_op jit(solution)/shard_map/dynamic_update_slice | solution.py:126
  1007.5 9.3 copy.44
  1016.8 92.3 %dynamic_update_slice.54 = f32[2,2,128,8192]{2,3,0,1:T(8,128)} dynamic-update-slice(f32[2,2,128,8192]{2,3,0,1:T(8,128)} %dynamic_update_slice.53, f32[2,2,8,8192]{2,3,0,1:T(8,128)} %copy.44, s32[]{:T(128)} %constant.44.clone.1, s32[]{:T(128)} %constant.44.clone.1, s32[]{:T(128)S(6)} %select_n.200, s32[]{:T(128)} %constant.44.clone.1) | dynamic-update-slice | bytes 2097156 | tf_op jit(solution)/shard_map/dynamic_update_slice | solution.py:126
  1109.0 9.3 copy.45
  1118.3 92.3 %dynamic_update_slice.55 = f32[2,2,128,8192]{2,3,0,1:T(8,128)} dynamic-update-slice(f32[2,2,128,8192]{2,3,0,1:T(8,128)} %dynamic_update_slice.54, f32[2,2,8,8192]{2,3,0,1:T(8,128)} %copy.45, s32[]{:T(128)} %constant.44.clone.1, s32[]{:T(128)} %constant.44.clone.1, s32[]{:T(128)S(6)} %select_n.202, s32[]{:T(128)} %constant.44.clone.1) | dynamic-update-slice | bytes 2097156 | tf_op jit(solution)/shard_map/dynamic_update_slice | solution.py:126
  1210.5 9.3 copy.46
  1219.8 92.3 %dynamic_update_slice.56 = f32[2,2,128,8192]{2,3,0,1:T(8,128)} dynamic-update-slice(f32[2,2,128,8192]{2,3,0,1:T(8,128)} %dynamic_update_slice.55, f32[2,2,8,8192]{2,3,0,1:T(8,128)} %copy.46, s32[]{:T(128)} %constant.44.clone.1, s32[]{:T(128)} %constant.44.clone.1, s32[]{:T(128)S(6)} %select_n.204, s32[]{:T(128)} %constant.44.clone.1) | dynamic-update-slice | bytes 2097156 | tf_op jit(solution)/shard_map/dynamic_update_slice | solution.py:126
  1312.1 9.3 copy.47
  1321.4 92.3 %dynamic_update_slice.57 = f32[2,2,128,8192]{2,3,0,1:T(8,128)} dynamic-update-slice(f32[2,2,128,8192]{2,3,0,1:T(8,128)} %dynamic_update_slice.56, f32[2,2,8,8192]{2,3,0,1:T(8,128)} %copy.47, s32[]{:T(128)} %constant.44.clone.1, s32[]{:T(128)} %constant.44.clone.1, s32[]{:T(128)S(6)} %select_n.206, s32[]{:T(128)} %constant.44.clone.1) | dynamic-update-slice | bytes 2097156 | tf_op jit(solution)/shard_map/dynamic_update_slice | solution.py:126
  1413.6 9.5 copy.48
  1423.1 92.3 %dynamic_update_slice.58 = f32[2,2,128,8192]{2,3,0,1:T(8,128)} dynamic-update-slice(f32[2,2,128,8192]{2,3,0,1:T(8,128)} %dynamic_update_slice.57, f32[2,2,8,8192]{2,3,0,1:T(8,128)} %copy.48, s32[]{:T(128)} %constant.44.clone.1, s32[]{:T(128)} %constant.44.clone.1, s32[]{:T(128)S(6)} %select_n.208, s32[]{:T(128)} %constant.44.clone.1) | dynamic-update-slice | bytes 2097156 | tf_op jit(solution)/shard_map/dynamic_update_slice | solution.py:126
  1515.4 9.3 copy.49
  1524.7 92.3 %dynamic_update_slice.59 = f32[2,2,128,8192]{2,3,0,1:T(8,128)} dynamic-update-slice(f32[2,2,128,8192]{2,3,0,1:T(8,128)} %dynamic_update_slice.58, f32[2,2,8,8192]{2,3,0,1:T(8,128)} %copy.49, s32[]{:T(128)} %constant.44.clone.1, s32[]{:T(128)} %constant.44.clone.1, s32[]{:T(128)S(6)} %select_n.210, s32[]{:T(128)} %constant.44.clone.1) | dynamic-update-slice | bytes 2097156 | tf_op jit(solution)/shard_map/dynamic_update_slice | solution.py:126
  1616.9 9.3 copy.50
  1626.2 92.3 %dynamic_update_slice.60 = f32[2,2,128,8192]{2,3,0,1:T(8,128)} dynamic-update-slice(f32[2,2,128,8192]{2,3,0,1:T(8,128)} %dynamic_update_slice.59, f32[2,2,8,8192]{2,3,0,1:T(8,128)} %copy.50, s32[]{:T(128)} %constant.44.clone.1, s32[]{:T(128)} %constant.44.clone.1, s32[]{:T(128)S(6)} %select_n.212, s32[]{:T(128)} %constant.44.clone.1) | dynamic-update-slice | bytes 2097156 | tf_op jit(solution)/shard_map/dynamic_update_slice | solution.py:126
  1718.5 9.3 copy.51
  1727.8 92.3 %dynamic_update_slice.61 = f32[2,2,128,8192]{2,3,0,1:T(8,128)} dynamic-update-slice(f32[2,2,128,8192]{2,3,0,1:T(8,128)} %dynamic_update_slice.60, f32[2,2,8,8192]{2,3,0,1:T(8,128)} %copy.51, s32[]{:T(128)} %constant.44.clone.1, s32[]{:T(128)} %constant.44.clone.1, s32[]{:T(128)S(6)} %select_n.214, s32[]{:T(128)} %constant.44.clone.1) | dynamic-update-slice | bytes 2097156 | tf_op jit(solution)/shard_map/dynamic_update_slice | solution.py:126
  1820.0 9.3 copy.52
  1829.3 92.3 %dynamic_update_slice.62 = f32[2,2,128,8192]{2,3,0,1:T(8,128)} dynamic-update-slice(f32[2,2,128,8192]{2,3,0,1:T(8,128)} %dynamic_update_slice.61, f32[2,2,8,8192]{2,3,0,1:T(8,128)} %copy.52, s32[]{:T(128)} %constant.44.clone.1, s32[]{:T(128)} %constant.44.clone.1, s32[]{:T(128)S(6)} %select_n.216, s32[]{:T(128)} %constant.44.clone.1) | dynamic-update-slice | bytes 2097156 | tf_op jit(solution)/shard_map/dynamic_update_slice | solution.py:126
  1921.6 9.3 copy.53
  1930.9 92.3 %dynamic_update_slice.63 = f32[2,2,128,8192]{2,3,0,1:T(8,128)} dynamic-update-slice(f32[2,2,128,8192]{2,3,0,1:T(8,128)} %dynamic_update_slice.62, f32[2,2,8,8192]{2,3,0,1:T(8,128)} %copy.53, s32[]{:T(128)} %constant.44.clone.1, s32[]{:T(128)} %constant.44.clone.1, s32[]{:T(128)S(6)} %select_n.218, s32[]{:T(128)} %constant.44.clone.1) | dynamic-update-slice | bytes 2097156 | tf_op jit(solution)/shard_map/dynamic_update_slice | solution.py:126
  2023.2 17.1 fusion.3
  2041.7 6.7 fusion.11
  2051.9 11.2 copy.54
  2063.1 8.9 all-to-all-start.2
  2072.1 90.1 %all-to-all-done.2 = bf16[2,2,128,4096]{3,0,1,2:T(2,128)(2,1)} async-done(((bf16[2,2,128,4096]{3,0,1,2:T(2,128)(2,1)}), bf16[2,2,128,4096]{3,0,1,2:T(2,128)(2,1)}, u32[]{:S(2)}, u32[]{:S(2)}) %all-to-all-start.2) | async-done | bytes 4194336 | tf_op jit(solution)/shard_map/all_to_all | solution.py:132
  2162.2 5.1 copy.73
  2173.8 7.1 all-to-all-start.3
  2182.4 23.4 %all-to-all-done.3 = bf16[16,8,4096]{2,1,0:T(8,128)(2,1)} async-done(((bf16[16,8,4096]{2,1,0:T(8,128)(2,1)}), bf16[16,8,4096]{2,1,0:T(8,128)(2,1)}, u32[]{:S(2)}, u32[]{:S(2)}) %all-to-all-start.3) | async-done | bytes 1048608 | tf_op jit(solution)/shard_map/all_to_all | solution.py:136
  2205.9 3.2 fusion.20
  (110 shorter events, 56.2 us)
Async XLA Ops:
  1.9 23.0 %collective-permute-start = (bf16[3,2,4096]{2,1,0:T(2,128)(2,1)S(1)}, bf16[3,2,4096]{2,1,0:T(2,128)(2,1)S(1)}, u32[]{:S(2)}, u32[]{:S(2)}) collective-permute-start(bf16[3,2,4096]{2,1,0:T(2,128)(2,1)S(1)} %pad_maximum_fusion.6), channel_id=1, source_target_pairs={{0,1},{1,2},{2,3},{3,4},{4,5},{5,6},{6,7},{7,8},{8,9},{9,10},{10,1... | collective-permute-start | bytes 147464 | tf_op jit(solution)/shard_map/ppermute | solution.py:13
  9.2 15.0 copy-start.14
  16.9 8.7 copy-start.4
  16.9 8.9 copy-start.5
  18.8 30.1 %all-to-all-start.1 = ((bf16[16,2,16384]{2,1,0:T(2,128)(2,1)}), bf16[16,2,16384]{2,1,0:T(2,128)(2,1)S(1)}, u32[]{:S(2)}, u32[]{:S(2)}) async-start(bf16[16,2,16384]{2,1,0:T(2,128)(2,1)} %reshape.316), calls=%async_computation.1 | async-start | bytes 2097152 | tf_op jit(solution)/shard_map/all_to_all | solution.py:103
  27.5 1.0 copy-start.2
  48.9 30.1 %all-to-all-start = ((bf16[16,2,16384]{2,1,0:T(2,128)(2,1)}), bf16[16,2,16384]{2,1,0:T(2,128)(2,1)}, u32[]{:S(2)}, u32[]{:S(2)}) async-start(bf16[16,2,16384]{2,1,0:T(2,128)(2,1)} %reshape.318), calls=%async_computation | async-start | bytes 2097152 | tf_op jit(solution)/shard_map/all_to_all | solution.py:100
  99.4 11.7 slice-start
  99.4 11.7 slice-start.1
  126.5 4.9 copy-start
  126.5 7.4 copy-start.1
  128.9 11.7 collective-permute-start.1
  128.9 24.5 %collective-permute-start.2 = (f32[2,2,8,8192]{3,2,1,0:T(8,128)}, f32[2,2,8,8192]{3,2,1,0:T(8,128)}, u32[]{:S(2)}, u32[]{:S(2)}) collective-permute-start(f32[2,2,8,8192]{3,2,1,0:T(8,128)} %get-tuple-element.12), channel_id=1, source_target_pairs={{0,2},{1,3},{2,0},{3,1},{4,6},{5,7},{6,4},{7,5},{8,10},{9,11},{10,... | collective-permute-start | bytes 3145736 | tf_op jit(solution)/shard_map/ppermute | solution.py:125
  130.3 46.5 %collective-permute-start.3 = (f32[2,2,8,8192]{3,2,1,0:T(8,128)}, f32[2,2,8,8192]{3,2,1,0:T(8,128)S(1)}, u32[]{:S(2)}, u32[]{:S(2)}) collective-permute-start(f32[2,2,8,8192]{3,2,1,0:T(8,128)} %get-tuple-element.13), channel_id=1, source_target_pairs={{0,3},{1,2},{2,1},{3,0},{4,7},{5,6},{6,5},{7,4},{8,11},{9,10},{10,... | collective-permute-start | bytes 3145736 | tf_op jit(solution)/shard_map/ppermute | solution.py:125
  131.1 46.9 %collective-permute-start.4 = (f32[2,2,8,8192]{3,2,1,0:T(8,128)}, f32[2,2,8,8192]{3,2,1,0:T(8,128)S(1)}, u32[]{:S(2)}, u32[]{:S(2)}) collective-permute-start(f32[2,2,8,8192]{3,2,1,0:T(8,128)} %get-tuple-element.14), channel_id=1, source_target_pairs={{0,4},{1,5},{2,6},{3,7},{4,0},{5,1},{6,2},{7,3},{8,12},{9,13},{10,... | collective-permute-start | bytes 3145736 | tf_op jit(solution)/shard_map/ppermute | solution.py:125
  136.5 42.5 %collective-permute-start.5 = (f32[2,2,8,8192]{3,2,1,0:T(8,128)}, f32[2,2,8,8192]{3,2,1,0:T(8,128)}, u32[]{:S(2)}, u32[]{:S(2)}) collective-permute-start(f32[2,2,8,8192]{3,2,1,0:T(8,128)} %get-tuple-element.16), channel_id=1, source_target_pairs={{0,5},{1,4},{2,7},{3,6},{4,1},{5,0},{6,3},{7,2},{8,13},{9,12},{10,... | collective-permute-start | bytes 3145736 | tf_op jit(solution)/shard_map/ppermute | solution.py:125
  136.5 4.1 copy-start.9
  136.6 16.9 copy-start.8
  136.6 40.3 %copy-start.7 = (f32[2,2,8,8192]{3,2,1,0:T(8,128)S(1)}, f32[2,2,8,8192]{3,2,1,0:T(8,128)}, u32[]{:S(2)}) copy-start(f32[2,2,8,8192]{3,2,1,0:T(8,128)} %get-tuple-element.19) | copy-start | bytes 3145732
  136.6 41.4 %copy-start.6 = (f32[2,2,8,8192]{3,2,1,0:T(8,128)S(1)}, f32[2,2,8,8192]{3,2,1,0:T(8,128)}, u32[]{:S(2)}) copy-start(f32[2,2,8,8192]{3,2,1,0:T(8,128)} %get-tuple-element.20) | copy-start | bytes 3145732
  140.7 103.5 %collective-permute-start.6 = (f32[2,2,8,8192]{3,2,1,0:T(8,128)S(1)}, f32[2,2,8,8192]{3,2,1,0:T(8,128)}, u32[]{:S(2)}, u32[]{:S(2)}) collective-permute-start(f32[2,2,8,8192]{3,2,1,0:T(8,128)S(1)} %copy-done.9), channel_id=1, source_target_pairs={{0,6},{1,7},{2,4},{3,5},{4,2},{5,3},{6,0},{7,1},{8,14},{9,15},{10,... | collective-permute-start | bytes 3145736 | tf_op jit(solution)/shard_map/ppermute | solution.py:125
  153.4 113.1 %collective-permute-start.7 = (f32[2,2,8,8192]{3,2,1,0:T(8,128)S(1)}, f32[2,2,8,8192]{3,2,1,0:T(8,128)}, u32[]{:S(2)}, u32[]{:S(2)}) collective-permute-start(f32[2,2,8,8192]{3,2,1,0:T(8,128)S(1)} %copy-done.8), channel_id=1, source_target_pairs={{0,7},{1,6},{2,5},{3,4},{4,3},{5,2},{6,1},{7,0},{8,15},{9,14},{10,... | collective-permute-start | bytes 3145736 | tf_op jit(solution)/shard_map/ppermute | solution.py:125
  176.9 90.2 %collective-permute-start.8 = (f32[2,2,8,8192]{3,2,1,0:T(8,128)S(1)}, f32[2,2,8,8192]{3,2,1,0:T(8,128)}, u32[]{:S(2)}, u32[]{:S(2)}) collective-permute-start(f32[2,2,8,8192]{3,2,1,0:T(8,128)S(1)} %copy-done.7), channel_id=1, source_target_pairs={{0,8},{1,9},{2,10},{3,11},{4,12},{5,13},{6,14},{7,15},{8,0},{9,1},... | collective-permute-start | bytes 3145736 | tf_op jit(solution)/shard_map/ppermute | solution.py:125
  178.0 92.7 %collective-permute-start.9 = (f32[2,2,8,8192]{3,2,1,0:T(8,128)S(1)}, f32[2,2,8,8192]{3,2,1,0:T(8,128)}, u32[]{:S(2)}, u32[]{:S(2)}) collective-permute-start(f32[2,2,8,8192]{3,2,1,0:T(8,128)S(1)} %copy-done.6), channel_id=1, source_target_pairs={{0,9},{1,8},{2,11},{3,10},{4,13},{5,12},{6,15},{7,14},{8,1},{9,0},... | collective-permute-start | bytes 3145736 | tf_op jit(solution)/shard_map/ppermute | solution.py:125
  179.1 223.9 %collective-permute-start.10 = (f32[2,2,8,8192]{3,2,1,0:T(8,128)S(1)}, f32[2,2,8,8192]{3,2,1,0:T(8,128)}, u32[]{:S(2)}, u32[]{:S(2)}) collective-permute-start(f32[2,2,8,8192]{3,2,1,0:T(8,128)S(1)} %get-tuple-element.22), channel_id=1, source_target_pairs={{0,10},{1,11},{2,8},{3,9},{4,14},{5,15},{6,12},{7,13},{8,2},{9,3},... | collective-permute-start | bytes 3145736 | tf_op jit(solution)/shard_map/ppermute | solution.py:125
  244.1 1271.2 %collective-permute-start.11 = (f32[2,2,8,8192]{3,2,1,0:T(8,128)}, f32[2,2,8,8192]{3,2,1,0:T(8,128)}, u32[]{:S(2)}, u32[]{:S(2)}) collective-permute-start(f32[2,2,8,8192]{3,2,1,0:T(8,128)} %get-tuple-element.23), channel_id=1, source_target_pairs={{0,11},{1,10},{2,9},{3,8},{4,15},{5,14},{6,13},{7,12},{8,3},{9,2},... | collective-permute-start | bytes 3145736 | tf_op jit(solution)/shard_map/ppermute | solution.py:125
  266.6 1350.3 %collective-permute-start.12 = (f32[2,2,8,8192]{3,2,1,0:T(8,128)}, f32[2,2,8,8192]{3,2,1,0:T(8,128)}, u32[]{:S(2)}, u32[]{:S(2)}) collective-permute-start(f32[2,2,8,8192]{3,2,1,0:T(8,128)} %get-tuple-element.24), channel_id=1, source_target_pairs={{0,12},{1,13},{2,14},{3,15},{4,8},{5,9},{6,10},{7,11},{8,4},{9,5},... | collective-permute-start | bytes 3145736 | tf_op jit(solution)/shard_map/ppermute | solution.py:125
  267.1 1451.4 %collective-permute-start.13 = (f32[2,2,8,8192]{3,2,1,0:T(8,128)}, f32[2,2,8,8192]{3,2,1,0:T(8,128)}, u32[]{:S(2)}, u32[]{:S(2)}) collective-permute-start(f32[2,2,8,8192]{3,2,1,0:T(8,128)} %get-tuple-element.21), channel_id=1, source_target_pairs={{0,13},{1,12},{2,15},{3,14},{4,9},{5,8},{6,11},{7,10},{8,5},{9,4},... | collective-permute-start | bytes 3145736 | tf_op jit(solution)/shard_map/ppermute | solution.py:125
  270.7 1549.3 %collective-permute-start.14 = (f32[2,2,8,8192]{3,2,1,0:T(8,128)}, f32[2,2,8,8192]{3,2,1,0:T(8,128)}, u32[]{:S(2)}, u32[]{:S(2)}) collective-permute-start(f32[2,2,8,8192]{3,2,1,0:T(8,128)} %get-tuple-element.15), channel_id=1, source_target_pairs={{0,14},{1,15},{2,12},{3,13},{4,10},{5,11},{6,8},{7,9},{8,6},{9,7},... | collective-permute-start | bytes 3145736 | tf_op jit(solution)/shard_map/ppermute | solution.py:125
  403.0 1518.6 %collective-permute-start.15 = (f32[2,2,8,8192]{3,2,1,0:T(8,128)}, f32[2,2,8,8192]{3,2,1,0:T(8,128)}, u32[]{:S(2)}, u32[]{:S(2)}) collective-permute-start(f32[2,2,8,8192]{3,2,1,0:T(8,128)} %get-tuple-element.9), channel_id=1, source_target_pairs={{0,15},{1,14},{2,13},{3,12},{4,11},{5,10},{6,9},{7,8},{8,7},{9,6},... | collective-permute-start | bytes 3145736 | tf_op jit(solution)/shard_map/ppermute | solution.py:125
  1930.9 92.3 %copy-start.12 = (f32[1,128,2,128]{3,1,2,0:T(8,128)S(1)}, f32[1,128,2,128]{3,1,2,0:T(8,128)}, u32[]{:S(2)}) copy-start(f32[1,128,2,128]{3,1,2,0:T(8,128)} %get-tuple-element.40) | copy-start | bytes 393220
  1930.9 92.3 %copy-start.13 = (f32[1,128,2,128]{3,1,2,0:T(8,128)S(1)}, f32[1,128,2,128]{3,1,2,0:T(8,128)}, u32[]{:S(2)}) copy-start(f32[1,128,2,128]{3,1,2,0:T(8,128)} %get-tuple-element.41) | copy-start | bytes 393220
  2040.3 1.4 copy-start.10
  2040.3 1.4 copy-start.11
  2041.6 6.8 copy-start.20
  2041.7 6.8 copy-start.21
  2063.1 99.1 %all-to-all-start.2 = ((bf16[2,2,128,4096]{3,0,1,2:T(2,128)(2,1)}), bf16[2,2,128,4096]{3,0,1,2:T(2,128)(2,1)}, u32[]{:S(2)}, u32[]{:S(2)}) async-start(bf16[2,2,128,4096]{3,0,1,2:T(2,128)(2,1)} %copy.54), calls=%async_computation.2 | async-start | bytes 8388608 | tf_op jit(solution)/shard_map/all_to_all | solution.py:132
  2170.4 10.5 copy-start.18
  2172.2 33.6 %copy-start.3 = (bf16[128,4096]{1,0:T(8,128)(2,1)S(1)}, bf16[128,4096]{1,0:T(8,128)(2,1)}, u32[]{:S(2)}) copy-start(bf16[128,4096]{1,0:T(8,128)(2,1)} %copy-done.2) | copy-start | bytes 3145732
  2172.2 33.6 %copy-start.15 = (f32[1,1,4096]{2,1,0:T(1,128)S(1)}, f32[1,1,4096]{2,1,0:T(1,128)}, u32[]{:S(2)}) copy-start(f32[1,1,4096]{2,1,0:T(1,128)} %get-tuple-element.29) | copy-start | bytes 49156
  2172.2 33.6 %copy-start.16 = (f32[1,1,4096]{2,1,0:T(1,128)S(1)}, f32[1,1,4096]{2,1,0:T(1,128)}, u32[]{:S(2)}) copy-start(f32[1,1,4096]{2,1,0:T(1,128)} %get-tuple-element.34) | copy-start | bytes 49156
  2172.3 33.6 %copy-start.17 = (f32[1,1,4096]{2,1,0:T(1,128)S(1)}, f32[1,1,4096]{2,1,0:T(1,128)}, u32[]{:S(2)}) copy-start(f32[1,1,4096]{2,1,0:T(1,128)} %get-tuple-element.35) | copy-start | bytes 49156
  2172.3 33.6 %copy-start.19 = (f32[4096]{0:T(1024)S(1)}, f32[4096]{0:T(1024)}, u32[]{:S(2)}) copy-start(f32[4096]{0:T(1024)} %param.11) | copy-start | bytes 49156
  2173.8 32.0 %all-to-all-start.3 = ((bf16[16,8,4096]{2,1,0:T(8,128)(2,1)}), bf16[16,8,4096]{2,1,0:T(8,128)(2,1)}, u32[]{:S(2)}, u32[]{:S(2)}) async-start(bf16[16,8,4096]{2,1,0:T(8,128)(2,1)} %bitcast.56), calls=%async_computation.3 | async-start | bytes 2097152 | tf_op jit(solution)/shard_map/all_to_all | solution.py:136
